TPU v7x, 128 devices: a whole 4x4x4 slice. The times are simulated.
128 devices in a mesh: dp: 4 (over x), seq: 16 (over y, z), mp: 2 (over core).
Axes of the slice: x: 4, y: 4, z: 4, core: 2. Of those that a mesh axis runs over, the one named last changes fastest.
Arguments:
- queries: bfloat16 [24576, 2048], P(('dp', 'seq'), 'mp'), may hold values from -64 to 64
- keys: bfloat16 [24576, 512], P(('dp', 'seq'), 'mp'), may hold values from -64 to 64
- values: bfloat16 [24576, 512], P(('dp', 'seq'), 'mp'), may hold values from -16 to 16
- offsets: int32 [24576], P(('dp', 'seq')), may hold values from 0 to 6143, as said below
- out_weight: bfloat16 [2048, 4096], P('mp'), may hold values from -0.125 to 0.125
- stream_in: bfloat16 [24576, 4096], P(('dp', 'seq'), 'mp'), may hold values from -64 to 64
- norm_gain: float32 [4096], replicated, may hold values from 0.1 to 1.9
- head_weight: bfloat16 [65536, 4096], P(('dp', 'seq', 'mp')), may hold values from -15 to 15
- picks: int32 [1024], P(('dp', 'seq')), may hold values from 0 to 383
- targets: int32 [1024], replicated, may hold values from 0 to 65535
Outputs:
- stream_out: bfloat16 [24576, 4096], P(('dp', 'seq'), 'mp')
- logprob: float32 [1024], P(('dp', 'seq', 'mp'))
Inputs may be any that keep to these rules, and one draw needn't show every extreme that they name: Each pack is cut into two to four consecutive rollouts; offsets[t] is the first position of the rollout that holds t, so offsets[t] <= t % 6144, and t % 6144 - offsets[t] is at most 3071, reached in every pack.
All inputs are finite; a program needn't handle non-finite values.
Results may differ from a plain program's by a relative error of at most 0.013.
Values may be sent and summed in bfloat16 or wider, within the bound.
No kernel may reach another device: no remote copies, remote signals or barrier semaphores. Data moves between devices by JAX's collectives and lax.ppermute only.
A program may use at most 128 MiB of HBM per device.

v0:
```python
import math
import jax
import jax.numpy as jnp
from jax import lax
from jax.sharding import PartitionSpec as P

HD = 128
GROUP = 4


def rounded_term(left, right):
    term = jnp.dot(left, right, preferred_element_type=jnp.float32)
    term = lax.optimization_barrier(term.astype(jnp.bfloat16))
    return term.astype(jnp.float32)


def on_device(
    queries, keys, values, offsets, out_weight, stream_in, norm_gain, head_weight, picks, targets
):
    rows_dev = queries.shape[0]
    block_rows = min(512, rows_dev)
    heads_dev = queries.shape[1] // HD
    groups_dev = keys.shape[1] // HD
    scale = 1.0 / math.sqrt(HD)
    seq_count = lax.axis_size("seq")
    reach_len = rows_dev * seq_count // 2
    pack_base = lax.axis_index("seq") * rows_dev
    stacked = jnp.stack([keys, values])
    whole = lax.all_gather(stacked, "seq", axis=1, tiled=True)
    padded = jnp.pad(whole, ((0, 0), (reach_len, 0), (0, 0)))
    joined = lax.dynamic_slice(
        padded, (0, pack_base, 0), (2, reach_len + rows_dev, stacked.shape[2])
    )
    window = reach_len + block_rows
    block_count = rows_dev // block_rows

    def attend(item):
        block = item // groups_dev
        group = item % groups_dev
        first = block * block_rows
        q_part = lax.dynamic_slice(queries, (first, group * GROUP * HD), (block_rows, GROUP * HD))
        q_part = q_part.reshape(block_rows, GROUP, HD)
        kv_part = lax.dynamic_slice(joined, (0, first, group * HD), (2, window, HD))
        scores = (
            jnp.einsum("qha,ka->hqk", q_part, kv_part[0], preferred_element_type=jnp.float32)
            * scale
        )
        query_pos = pack_base + first + jnp.arange(block_rows, dtype=jnp.int32)
        key_pos = pack_base - reach_len + first + jnp.arange(window, dtype=jnp.int32)
        allowed = (key_pos[None, :] >= offsets[:, None]) & (key_pos[None, :] <= query_pos[:, None])
        scores = jnp.where(allowed[None], scores, -jnp.inf)
        top = jnp.max(scores, axis=-1, keepdims=True)
        weights = jnp.exp(scores - top)
        probs = (weights / jnp.sum(weights, axis=-1, keepdims=True)).astype(jnp.bfloat16)
        mixed = jnp.einsum("hqk,ka->qha", probs, kv_part[1], preferred_element_type=jnp.float32)
        return mixed.astype(jnp.bfloat16).reshape(block_rows, GROUP * HD)

    pieces = lax.map(attend, jnp.arange(block_count * groups_dev, dtype=jnp.int32))
    context = pieces.reshape(block_count, groups_dev, block_rows, GROUP * HD).transpose(0, 2, 1, 3)
    context = context.reshape(rows_dev, heads_dev * HD)
    partial_terms = rounded_term(context, out_weight)
    branch = lax.psum_scatter(
        partial_terms.astype(jnp.bfloat16), "mp", scatter_dimension=1, tiled=True
    ).astype(jnp.float32)
    stream_out = (stream_in.astype(jnp.float32) + branch).astype(jnp.bfloat16)
    chosen = jnp.take(stream_out, picks, axis=0)
    full_rows = lax.all_gather(chosen, "mp", axis=1, tiled=True).astype(jnp.float32)
    inverse = lax.rsqrt(jnp.mean(full_rows * full_rows, axis=-1, keepdims=True) + 1e-05)
    normed = (full_rows * inverse * norm_gain).astype(jnp.bfloat16)
    logits = lax.dot_general(
        lax.all_gather(normed, ("dp", "seq"), axis=0, tiled=True),
        head_weight,
        (((1,), (1,)), ((), ())),
        preferred_element_type=jnp.float32,
    )
    vocab_rows = head_weight.shape[0]
    flat_index = lax.axis_index(("dp", "seq", "mp"))
    vocab_first = flat_index * vocab_rows
    hit = targets[:, None] == vocab_first + jnp.arange(vocab_rows, dtype=jnp.int32)[None, :]
    target_part = jnp.sum(jnp.where(hit, logits, 0.0), axis=-1)
    local_top = jnp.max(logits, axis=-1)
    out_rows = logits.shape[0] // lax.axis_size(("dp", "seq", "mp"))
    own_first = flat_index * out_rows
    top_all = lax.pmax(local_top, ("dp", "seq", "mp"))
    expsum = jnp.sum(jnp.exp(logits - top_all[:, None]), axis=-1)
    total, target_logit = (
        lax.psum_scatter(expsum, ("dp", "seq", "mp"), scatter_dimension=0, tiled=True),
        lax.psum_scatter(target_part, ("dp", "seq", "mp"), scatter_dimension=0, tiled=True),
    )
    top_own = lax.dynamic_slice_in_dim(top_all, own_first, out_rows)
    logprob = target_logit - top_own - jnp.log(total)
    return (stream_out, logprob)


def solution(mesh):
    placed = (
        P(("dp", "seq"), "mp"),
        P(("dp", "seq"), "mp"),
        P(("dp", "seq"), "mp"),
        P(("dp", "seq")),
        P("mp", None),
        P(("dp", "seq"), "mp"),
        P(),
        P(("dp", "seq", "mp"), None),
        P(("dp", "seq")),
        P(),
    )
    return jax.shard_map(
        on_device,
        mesh=mesh,
        in_specs=placed,
        out_specs=(P(("dp", "seq"), "mp"), P(("dp", "seq", "mp"))),
        check_vma=False,
    )
```

profile of v0, /device:TPU:1, one launch (start us, length us, event | category | flops | bytes accessed | tf_op | source)
XLA Modules:
  0.0 392.5 jit_solution(1795394309466374496)
XLA Ops:
  7.2 1.8 pad_maximum_fusion
  9.2 65.4 %all-gather.3.cloned.1.call-done = bf16[2,6144,256]{2,1,0:T(8,128)(2,1)} async-done(((bf16[2,384,256]{2,1,0:T(8,128)(2,1)}), bf16[2,6144,256]{2,1,0:T(8,128)(2,1)}) %all-gather.3.cloned.1.call-update) | async-done | bytes 6291472 | tf_op jit(solution)/shard_map/all_gather | solution.py:29
  74.6 3.6 pad_dynamic-slice_fusion
  78.2 56.9 %while.12 = (s32[]{:T(128)}, bf16[2,384,512]{1,2,0:T(8,128)(2,1)}, s32[2]{0:T(128)S(1)}, bf16[2,3456,256]{2,1,0:T(8,128)(2,1)}, s32[]{:T(128)}, /*index=5*/s32[3...) while((s32[]{:T(128)}, bf16[2,384,512]{1,2,0:T(8,128)(2,1)}, ...), condition=%wide.region_3.4_spmd, body=%wide.region_0.3_spmd.sunk | while | flops 2753944576 | bytes 56373324 | solution.py:58
  78.2 0.7 dynamic_slice.35
  81.7 1.7 compare_and_fusion.3
  83.7 13.0 %fusion.33 = (f32[4,384]{1,0:T(4,128)S(1)}, f32[4,384,3456]{1,2,0:T(8,128)}) fusion(pred[384,3456]{0,1:T(8,128)(4,1)S(1)} %compare_and_fusion.3, bf16[384,4,128]{0,2,1:T(8,128)(2,1)S(1)} %bitcast.61, bf16[2,3456,256]{2,1,0:T(8,128)(2,1)} %get-tuple-element.235, s32[]{:T(128)S(6)} %select_n.88), kind=kOutput, calls=%fused_computation.45.clone.1 | convolution fusion | flops 1380191616 | bytes 23844868 | tf_op jit(solution)/shard_map/while/body/eval_jaxpr/sub | solution.py:53
  96.7 9.0 %fusion.34 = bf16[128,4,384]{2,0,1:T(8,128)(2,1)S(1)} fusion(f32[4,384,3456]{1,2,0:T(8,128)} %get-tuple-element.194, f32[4,384]{1,0:T(4,128)S(1)} %get-tuple-element.195, bf16[2,3456,256]{2,1,0:T(8,128)(2,1)} %get-tuple-element.235, s32[]{:T(128)S(6)} %add.164, s32[]{:T(128)S(6)} %select_n.88), kind=kOutput, calls=%fused_computation.12.clone.1 | convolution fusion | flops 1369767936 | bytes 22517768 | tf_op jit(solution)/shard_map/while/body/eval_jaxpr/hqk,ka->qha/dot_general | solution.py:55
  105.8 0.9 copy-done.7
  106.7 0.7 dynamic_slice.35
  110.1 1.7 compare_and_fusion.3
  112.1 13.0 %fusion.33 = (f32[4,384]{1,0:T(4,128)S(1)}, f32[4,384,3456]{1,2,0:T(8,128)}) fusion(pred[384,3456]{0,1:T(8,128)(4,1)S(1)} %compare_and_fusion.3, bf16[384,4,128]{0,2,1:T(8,128)(2,1)S(1)} %bitcast.61, bf16[2,3456,256]{2,1,0:T(8,128)(2,1)} %get-tuple-element.235, s32[]{:T(128)S(6)} %select_n.88), kind=kOutput, calls=%fused_computation.45.clone.1 | convolution fusion | flops 1380191616 | bytes 23844868 | tf_op jit(solution)/shard_map/while/body/eval_jaxpr/sub | solution.py:53
  125.1 9.0 %fusion.34 = bf16[128,4,384]{2,0,1:T(8,128)(2,1)S(1)} fusion(f32[4,384,3456]{1,2,0:T(8,128)} %get-tuple-element.194, f32[4,384]{1,0:T(4,128)S(1)} %get-tuple-element.195, bf16[2,3456,256]{2,1,0:T(8,128)(2,1)} %get-tuple-element.235, s32[]{:T(128)S(6)} %add.164, s32[]{:T(128)S(6)} %select_n.88), kind=kOutput, calls=%fused_computation.12.clone.1 | convolution fusion | flops 1369767936 | bytes 22517768 | tf_op jit(solution)/shard_map/while/body/eval_jaxpr/hqk,ka->qha/dot_general | solution.py:55
  134.3 0.9 copy-done.7
  135.1 8.8 %convolution_convert_fusion = bf16[384,4096]{1,0:T(8,128)(2,1)} fusion(bf16[384,1024]{0,1:T(8,128)(2,1)} %bitcast.65, bf16[1024,4096]{1,0:T(8,128)(2,1)} %param.16), kind=kOutput, calls=%fused_computation.26 | convolution fusion | flops 3222798336 | bytes 12320768 | tf_op jit(solution)/shard_map/dot_general | solution.py:12
  144.2 14.6 %reduce-scatter.2.cloned.1.call-done = bf16[384,2048]{1,0:T(8,128)(2,1)} async-done(((bf16[384,4096]{1,0:T(8,128)(2,1)}), bf16[384,2048]{1,0:T(8,128)(2,1)}) %reduce-scatter.2.cloned.1.call-update) | async-done | bytes 1572880 | tf_op jit(solution)/shard_map/reduce_scatter | solution.py:62
  158.8 2.0 add_convert_fusion
  161.6 2.0 all_gather.10
  163.7 0.8 fusion.19
  164.5 79.4 %all-gather.5.cloned.1.call-done = bf16[1024,4096]{1,0:T(8,128)(2,1)} async-done(((bf16[16,4096]{1,0:T(8,128)(2,1)}), bf16[1024,4096]{1,0:T(8,128)(2,1)}) %all-gather.5.cloned.1.call-update) | async-done | bytes 8388624 | tf_op jit(solution)/shard_map/all_gather | solution.py:71
  243.9 10.5 %fusion.22 = (f32[1024]{0:T(1024)S(1)}, f32[1024,512]{0,1:T(8,128)}) fusion(bf16[1024,4096]{1,0:T(8,128)(2,1)} %all-gather.5.cloned.1.call-done, bf16[512,4096]{1,0:T(8,128)(2,1)} %param.19), kind=kOutput, calls=%fused_computation.46 | convolution fusion | flops 4295490560 | bytes 14684160 | tf_op jit(solution)/shard_map/dot_general | solution.py:70
  254.4 64.7 %pmax.7 = f32[1024]{0:T(1024)S(1)} all-reduce(f32[1024]{0:T(1024)S(1)} %get-tuple-element.141), channel_id=1, replica_groups=mesh['dp'=4,'seq'=16,'mp'=2] {'dp','seq','mp'}, use_global_device_ids=true, to_apply=%region_9.10 | all-reduce | flops 1024 | bytes 8192 | tf_op jit(solution)/shard_map/pmax | solution.py:84
  319.1 2.1 select_reduce_fusion
  321.1 64.3 %all-reduce.3 = (f32[1024]{0:T(1024)S(1)}, f32[1024]{0:T(1024)S(1)}) all-reduce(f32[1024]{0:T(1024)S(1)} %get-tuple-element.120, f32[1024]{0:T(1024)S(1)} %get-tuple-element.119), channel_id=4, replica_groups=mesh['dp'=4,'seq'=16,'mp'=2] {'dp','seq','mp'}, use_global_device_ids=true, to_apply=%region_11.12.clone | all-reduce | flops 2048 | bytes 16384
  (47 shorter events, 2.5 us)
Async XLA Ops:
  7.2 67.4 %all-gather.3.cloned.1.call-start = ((), (), s32[]{:S(2)}) async-start(), calls=%async_computation.1 | async-start | bytes 6684672 | tf_op jit(solution)/shard_map/all_gather | solution.py:29
  9.1 149.8 %reduce-scatter.2.cloned.1.call-start = ((), (), s32[]{:S(2)}) async-start(), calls=%async_computation.2 | async-start | bytes 4718592 | tf_op jit(solution)/shard_map/reduce_scatter | solution.py:62
  9.1 69.1 %copy-start = (bf16[384,1024]{1,0:T(8,128)(2,1)S(1)}, bf16[384,1024]{1,0:T(8,128)(2,1)}, u32[]{:S(2)}) copy-start(bf16[384,1024]{1,0:T(8,128)(2,1)} %param.12) | copy-start | bytes 2359300
  9.1 69.1 %copy-start.3 = (s32[384]{0:T(512)S(1)}, s32[384]{0:T(512)}, u32[]{:S(2)}) copy-start(s32[384]{0:T(512)} %param.15) | copy-start | bytes 4612
  96.7 9.0 %copy-start.6 = (bf16[2,384,512]{1,2,0:T(8,128)(2,1)S(1)}, bf16[2,384,512]{1,2,0:T(8,128)(2,1)}, u32[]{:S(2)}) copy-start(bf16[2,384,512]{1,2,0:T(8,128)(2,1)} %get-tuple-element.215) | copy-start | bytes 2359300 | tf_op jit(solution)/shard_map/while
  105.8 0.9 copy-start.7
  125.1 9.0 %copy-start.6 = (bf16[2,384,512]{1,2,0:T(8,128)(2,1)S(1)}, bf16[2,384,512]{1,2,0:T(8,128)(2,1)}, u32[]{:S(2)}) copy-start(bf16[2,384,512]{1,2,0:T(8,128)(2,1)} %get-tuple-element.215) | copy-start | bytes 2359300 | tf_op jit(solution)/shard_map/while
  134.2 0.9 copy-start.7
  135.1 9.1 %copy-start.8 = (s32[16]{0:T(128)S(1)}, s32[16]{0:T(128)}, u32[]{:S(2)}) copy-start(s32[16]{0:T(128)} %param.20) | copy-start | bytes 196
  143.9 14.9 %copy-start.2 = (bf16[384,2048]{1,0:T(8,128)(2,1)S(1)}, bf16[384,2048]{1,0:T(8,128)(2,1)}, u32[]{:S(2)}) copy-start(bf16[384,2048]{1,0:T(8,128)(2,1)} %param.17) | copy-start | bytes 4718596
  143.9 19.8 %copy-start.4 = (f32[4096]{0:T(1024)S(1)}, f32[4096]{0:T(1024)}, u32[]{:S(2)}) copy-start(f32[4096]{0:T(1024)} %param.18) | copy-start | bytes 49156
  143.9 99.9 %all-gather.5.cloned.1.call-start = ((), (), s32[]{:S(2)}) async-start(), calls=%async_computation.3 | async-start | bytes 8519680 | tf_op jit(solution)/shard_map/all_gather | solution.py:71
  160.9 93.5 %copy-start.1 = (bf16[384,2048]{1,0:T(8,128)(2,1)}, bf16[384,2048]{1,0:T(8,128)(2,1)S(1)}, u32[]{:S(2)}) copy-start(bf16[384,2048]{1,0:T(8,128)(2,1)S(1)} %add_convert_fusion) | copy-start | bytes 4718596
  164.5 154.5 %copy-start.5 = (s32[1024]{0:T(1024)S(1)}, s32[1024]{0:T(1024)}, u32[]{:S(2)}) copy-start(s32[1024]{0:T(1024)} %param.21) | copy-start | bytes 12292
Sparse Core Ops, SparseCore 0:
  10.1 64.4 all-gather.2
  144.1 14.7 reduce-scatter.1
  164.6 79.2 all-gather.4
where the time goes:
time: 393 us
  waiting for transfers between devices  159 us (40%)
  blocking collectives  131 us (33%)
  matrix products  63.3 us (16%)
  between operations  13.9 us (4%)
  other arithmetic  10.9 us (3%)
  local copies, waits for them, and re-layouts  7.97 us (2%)
  loops' own time  5.79 us (1%)
    all_gather x1, waiting for transfers between devices, on_device(): lax.all_gather(normed, ('dp', 'seq'), axis=0, tiled=True)  79.4 us
    all_gather x1, waiting for transfers between devices, on_device(): whole = lax.all_gather(stacked, 'seq', axis=1, tiled=True)  65.4 us
    pmax x1, blocking collectives, on_device(): top_all = lax.pmax(local_top, ('dp', 'seq', 'mp'))  64.7 us
    unnamed x1, blocking collectives  64.3 us
    sub x2, matrix products, attend(): weights = jnp.exp(scores - top)  26.1 us
    dot_general x2, matrix products, attend(): jnp.einsum('hqk,ka->qha', probs, kv_part[1], preferred_element_type=jnp.f...  18 us
    reduce_scatter x1, waiting for transfers between devices, on_device(): lax.psum_scatter(partial_terms.astype(jnp.bfloat16), 'mp', scatter_dimens...  14.6 us
    dot_general x1, matrix products, on_device(): lax.dot_general(lax.all_gather(normed, ('dp', 'seq'), axis=0, tiled=True)...  10.5 us
  transfers between devices with their start and end apart: 3, of which 3 were waited for; matrix products, arithmetic and copies ran while one was open for 0% of the time, Pallas kernels for 0%

commit v1 on v0

--- a/solution.py
+++ b/solution.py
@@ -26,7 +26,8 @@
     reach_len = rows_dev * seq_count // 2
     pack_base = lax.axis_index("seq") * rows_dev
     stacked = jnp.stack([keys, values])
-    whole = lax.all_gather(stacked, "seq", axis=1, tiled=True)
+    repeated = jnp.stack([stacked] * lax.axis_size("seq"))
+    whole = jnp.concatenate(lax.all_to_all(repeated, "seq", 0, 0), axis=1)
     padded = jnp.pad(whole, ((0, 0), (reach_len, 0), (0, 0)))
     joined = lax.dynamic_slice(
         padded, (0, pack_base, 0), (2, reach_len + rows_dev, stacked.shape[2])

time: 393 us -> 450 us (1.15)
  waiting for transfers between devices: 159 us -> 201 us
  starting transfers between devices: 0.3 us -> 8.71 us
  local copies, waits for them, and re-layouts: 7.97 us -> 15.1 us
    all_to_all x0 -> x1, waiting for transfers between devices: none -> 98.5 us  [on_device(): whole = jnp.concatenate(lax.all_to_all(repeated, 'seq', 0, 0), axis=1)]
    all_gather x1 -> x0, waiting for transfers between devices: 65.4 us -> none  [on_device(): whole = lax.all_gather(stacked, 'seq', axis=1, tiled=True)]
    all_to_all x0 -> x1, starting transfers between devices: none -> 8.63 us  [on_device(): whole = jnp.concatenate(lax.all_to_all(repeated, 'seq', 0, 0), axis=1)]
    reduce_scatter x1, waiting for transfers between devices: 14.6 us -> 23.1 us  [on_device(): lax.psum_scatter(partial_terms.astype(jnp.bfloat16), 'mp', scatter_dimens...]
where the time goes in v1:
time: 450 us; the launch traced here: 449 us
  waiting for transfers between devices  201 us (45%)
  blocking collectives  131 us (29%)
  matrix products  63.3 us (14%)
  local copies, waits for them, and re-layouts  15.1 us (3%)
  between operations  14.2 us (3%)
  other arithmetic  10.1 us (2%)
  starting transfers between devices  8.71 us (2%)
  loops' own time  5.79 us (1%)
    all_to_all x1, waiting for transfers between devices, on_device(): whole = jnp.concatenate(lax.all_to_all(repeated, 'seq', 0, 0), axis=1)  98.5 us
    all_gather x1, waiting for transfers between devices, on_device(): lax.all_gather(normed, ('dp', 'seq'), axis=0, tiled=True)  79.4 us
    pmax x1, blocking collectives, on_device(): top_all = lax.pmax(local_top, ('dp', 'seq', 'mp'))  64.7 us
    unnamed x1, blocking collectives  64.3 us
    sub x2, matrix products, attend(): weights = jnp.exp(scores - top)  26.1 us
    reduce_scatter x1, waiting for transfers between devices, on_device(): lax.psum_scatter(partial_terms.astype(jnp.bfloat16), 'mp', scatter_dimens...  23.1 us
    dot_general x2, matrix products, attend(): jnp.einsum('hqk,ka->qha', probs, kv_part[1], preferred_element_type=jnp.f...  18 us
    dot_general x1, matrix products, on_device(): lax.dot_general(lax.all_gather(normed, ('dp', 'seq'), axis=0, tiled=True)...  10.5 us
  transfers between devices with their start and end apart: 3, of which 3 were waited for; matrix products, arithmetic and copies ran while one was open for 0% of the time, Pallas kernels for 0%

profile of v1, /device:TPU:1, one launch (start us, length us, event | category | flops | bytes accessed | tf_op | source)
XLA Modules:
  0.0 449.3 jit_solution(3709787078647884581)
XLA Ops:
  7.2 1.1 pad_maximum_fusion
  8.2 3.4 stack.11
  11.6 8.6 %all-to-all-start = ((bf16[16,2,384,256]{3,2,1,0:T(8,128)(2,1)}), bf16[16,2,384,256]{3,2,1,0:T(8,128)(2,1)}, u32[]{:S(2)}, u32[]{:S(2)}) async-start(bf16[16,2,384,256]{3,2,1,0:T(8,128)(2,1)} %stack.11), calls=%async_computation | async-start | bytes 12582912 | tf_op jit(solution)/shard_map/all_to_all | solution.py:30
  20.3 98.5 %all-to-all-done = bf16[16,2,384,256]{3,2,1,0:T(8,128)(2,1)} async-done(((bf16[16,2,384,256]{3,2,1,0:T(8,128)(2,1)}), bf16[16,2,384,256]{3,2,1,0:T(8,128)(2,1)}, u32[]{:S(2)}, u32[]{:S(2)}) %all-to-all-start) | async-done | bytes 6291488 | tf_op jit(solution)/shard_map/all_to_all | solution.py:30
  118.8 3.2 copy.25
  122.1 4.2 pad_dynamic-slice_fusion
  126.2 56.9 %while.12 = (s32[]{:T(128)}, bf16[2,384,512]{1,2,0:T(8,128)(2,1)}, s32[2]{0:T(128)S(1)}, bf16[2,3456,256]{2,1,0:T(8,128)(2,1)}, s32[]{:T(128)}, /*index=5*/s32[3...) while((s32[]{:T(128)}, bf16[2,384,512]{1,2,0:T(8,128)(2,1)}, ...), condition=%wide.region_3.4_spmd, body=%wide.region_0.3_spmd.sunk | while | flops 2753944576 | bytes 56373324 | solution.py:59
  129.7 1.7 compare_and_fusion.3
  131.7 13.0 %fusion.33 = (f32[4,384]{1,0:T(4,128)S(1)}, f32[4,384,3456]{1,2,0:T(8,128)}) fusion(pred[384,3456]{0,1:T(8,128)(4,1)S(1)} %compare_and_fusion.3, bf16[384,4,128]{0,2,1:T(8,128)(2,1)S(1)} %bitcast.65, bf16[2,3456,256]{2,1,0:T(8,128)(2,1)} %get-tuple-element.243, s32[]{:T(128)S(6)} %select_n.88), kind=kOutput, calls=%fused_computation.45.clone.1 | convolution fusion | flops 1380191616 | bytes 23844868 | tf_op jit(solution)/shard_map/while/body/eval_jaxpr/sub | solution.py:54
  144.7 9.0 %fusion.34 = bf16[128,4,384]{2,0,1:T(8,128)(2,1)S(1)} fusion(f32[4,384,3456]{1,2,0:T(8,128)} %get-tuple-element.202, f32[4,384]{1,0:T(4,128)S(1)} %get-tuple-element.203, bf16[2,3456,256]{2,1,0:T(8,128)(2,1)} %get-tuple-element.243, s32[]{:T(128)S(6)} %add.164, s32[]{:T(128)S(6)} %select_n.88), kind=kOutput, calls=%fused_computation.12.clone.1 | convolution fusion | flops 1369767936 | bytes 22517768 | tf_op jit(solution)/shard_map/while/body/eval_jaxpr/hqk,ka->qha/dot_general | solution.py:56
  153.8 0.9 copy-done.7
  158.2 1.7 compare_and_fusion.3
  160.2 13.0 %fusion.33 = (f32[4,384]{1,0:T(4,128)S(1)}, f32[4,384,3456]{1,2,0:T(8,128)}) fusion(pred[384,3456]{0,1:T(8,128)(4,1)S(1)} %compare_and_fusion.3, bf16[384,4,128]{0,2,1:T(8,128)(2,1)S(1)} %bitcast.65, bf16[2,3456,256]{2,1,0:T(8,128)(2,1)} %get-tuple-element.243, s32[]{:T(128)S(6)} %select_n.88), kind=kOutput, calls=%fused_computation.45.clone.1 | convolution fusion | flops 1380191616 | bytes 23844868 | tf_op jit(solution)/shard_map/while/body/eval_jaxpr/sub | solution.py:54
  173.2 9.0 %fusion.34 = bf16[128,4,384]{2,0,1:T(8,128)(2,1)S(1)} fusion(f32[4,384,3456]{1,2,0:T(8,128)} %get-tuple-element.202, f32[4,384]{1,0:T(4,128)S(1)} %get-tuple-element.203, bf16[2,3456,256]{2,1,0:T(8,128)(2,1)} %get-tuple-element.243, s32[]{:T(128)S(6)} %add.164, s32[]{:T(128)S(6)} %select_n.88), kind=kOutput, calls=%fused_computation.12.clone.1 | convolution fusion | flops 1369767936 | bytes 22517768 | tf_op jit(solution)/shard_map/while/body/eval_jaxpr/hqk,ka->qha/dot_general | solution.py:56
  182.3 0.9 copy-done.7
  183.2 8.8 %convolution_convert_fusion = bf16[384,4096]{1,0:T(8,128)(2,1)} fusion(bf16[384,1024]{0,1:T(8,128)(2,1)} %bitcast.69, bf16[1024,4096]{1,0:T(8,128)(2,1)} %param.16), kind=kOutput, calls=%fused_computation.26 | convolution fusion | flops 3222798336 | bytes 12320768 | tf_op jit(solution)/shard_map/dot_general | solution.py:12
  192.1 23.1 %reduce-scatter.2.cloned.1.call-done = bf16[384,2048]{1,0:T(8,128)(2,1)} async-done(((bf16[384,4096]{1,0:T(8,128)(2,1)}), bf16[384,2048]{1,0:T(8,128)(2,1)}) %reduce-scatter.2.cloned.1.call-update) | async-done | bytes 1572880 | tf_op jit(solution)/shard_map/reduce_scatter | solution.py:63
  215.1 2.0 add_convert_fusion
  217.8 2.2 all_gather.6
  221.0 79.4 %all-gather.2.cloned.1.call-done = bf16[1024,4096]{1,0:T(8,128)(2,1)} async-done(((bf16[16,4096]{1,0:T(8,128)(2,1)}), bf16[1024,4096]{1,0:T(8,128)(2,1)}) %all-gather.2.cloned.1.call-update) | async-done | bytes 8388624 | tf_op jit(solution)/shard_map/all_gather | solution.py:72
  300.4 10.5 %fusion.22 = (f32[1024]{0:T(1024)S(1)}, f32[1024,512]{0,1:T(8,128)}) fusion(bf16[1024,4096]{1,0:T(8,128)(2,1)} %all-gather.2.cloned.1.call-done, bf16[512,4096]{1,0:T(8,128)(2,1)} %param.19), kind=kOutput, calls=%fused_computation.46 | convolution fusion | flops 4295490560 | bytes 14684160 | tf_op jit(solution)/shard_map/dot_general | solution.py:71
  310.9 64.7 %pmax.7 = f32[1024]{0:T(1024)S(1)} all-reduce(f32[1024]{0:T(1024)S(1)} %get-tuple-element.149), channel_id=1, replica_groups=mesh['dp'=4,'seq'=16,'mp'=2] {'dp','seq','mp'}, use_global_device_ids=true, to_apply=%region_9.10 | all-reduce | flops 1024 | bytes 8192 | tf_op jit(solution)/shard_map/pmax | solution.py:85
  375.6 2.1 select_reduce_fusion
  377.7 64.3 %all-reduce.3 = (f32[1024]{0:T(1024)S(1)}, f32[1024]{0:T(1024)S(1)}) all-reduce(f32[1024]{0:T(1024)S(1)} %get-tuple-element.128, f32[1024]{0:T(1024)S(1)} %get-tuple-element.127), channel_id=4, replica_groups=mesh['dp'=4,'seq'=16,'mp'=2] {'dp','seq','mp'}, use_global_device_ids=true, to_apply=%region_11.12.clone | all-reduce | flops 2048 | bytes 16384
  (48 shorter events, 4.3 us)
Async XLA Ops:
  11.6 107.2 %all-to-all-start = ((bf16[16,2,384,256]{3,2,1,0:T(8,128)(2,1)}), bf16[16,2,384,256]{3,2,1,0:T(8,128)(2,1)}, u32[]{:S(2)}, u32[]{:S(2)}) async-start(bf16[16,2,384,256]{3,2,1,0:T(8,128)(2,1)} %stack.11), calls=%async_computation | async-start | bytes 12582912 | tf_op jit(solution)/shard_map/all_to_all | solution.py:30
  20.2 194.9 %reduce-scatter.2.cloned.1.call-start = ((), (), s32[]{:S(2)}) async-start(), calls=%async_computation.2 | async-start | bytes 4718592 | tf_op jit(solution)/shard_map/reduce_scatter | solution.py:63
  122.0 4.2 copy-start
  122.0 4.2 copy-start.3
  144.7 9.0 %copy-start.6 = (bf16[2,384,512]{1,2,0:T(8,128)(2,1)S(1)}, bf16[2,384,512]{1,2,0:T(8,128)(2,1)}, u32[]{:S(2)}) copy-start(bf16[2,384,512]{1,2,0:T(8,128)(2,1)} %get-tuple-element.223) | copy-start | bytes 2359300 | tf_op jit(solution)/shard_map/while
  153.8 0.9 copy-start.7
  173.2 9.0 %copy-start.6 = (bf16[2,384,512]{1,2,0:T(8,128)(2,1)S(1)}, bf16[2,384,512]{1,2,0:T(8,128)(2,1)}, u32[]{:S(2)}) copy-start(bf16[2,384,512]{1,2,0:T(8,128)(2,1)} %get-tuple-element.223) | copy-start | bytes 2359300 | tf_op jit(solution)/shard_map/while
  182.3 0.9 copy-start.7
  183.2 8.9 %copy-start.8 = (s32[16]{0:T(128)S(1)}, s32[16]{0:T(128)}, u32[]{:S(2)}) copy-start(s32[16]{0:T(128)} %param.20) | copy-start | bytes 196
  192.0 23.2 %copy-start.2 = (bf16[384,2048]{1,0:T(8,128)(2,1)S(1)}, bf16[384,2048]{1,0:T(8,128)(2,1)}, u32[]{:S(2)}) copy-start(bf16[384,2048]{1,0:T(8,128)(2,1)} %param.17) | copy-start | bytes 4718596
  192.0 28.2 %copy-start.4 = (f32[4096]{0:T(1024)S(1)}, f32[4096]{0:T(1024)}, u32[]{:S(2)}) copy-start(f32[4096]{0:T(1024)} %param.18) | copy-start | bytes 49156
  192.0 108.4 %all-gather.2.cloned.1.call-start = ((), (), s32[]{:S(2)}) async-start(), calls=%async_computation.3 | async-start | bytes 8519680 | tf_op jit(solution)/shard_map/all_gather | solution.py:72
  217.2 93.7 %copy-start.1 = (bf16[384,2048]{1,0:T(8,128)(2,1)}, bf16[384,2048]{1,0:T(8,128)(2,1)S(1)}, u32[]{:S(2)}) copy-start(bf16[384,2048]{1,0:T(8,128)(2,1)S(1)} %add_convert_fusion) | copy-start | bytes 4718596
  221.0 154.5 %copy-start.5 = (s32[1024]{0:T(1024)S(1)}, s32[1024]{0:T(1024)}, u32[]{:S(2)}) copy-start(s32[1024]{0:T(1024)} %param.21) | copy-start | bytes 12292
Sparse Core Ops, SparseCore 0:
  192.1 22.9 reduce-scatter.1
  221.1 79.2 all-gather.1
